TPU v7x, 256 devices: a whole 4x4x8 slice. The times are simulated.
256 devices in a mesh: dp: 8 (over x, core), expert: 32 (over z, y).
Axes of the slice: x: 4, y: 4, z: 8, core: 2. Of those that a mesh axis runs over, the one named last changes fastest.
Arguments:
- tokens: bfloat16 [8192, 7168], P('expert', 'dp'), may hold values from -6 to 6
- grad_out: bfloat16 [8192, 7168], P('expert', 'dp'), may hold values from -6 to 6
- route_ids: int32 [8192, 8], P('expert'), may hold values from 0 to 255, all different within a row; in each aligned block of 256 rows (0 to 255, 256 to 511, ...) at most 12 rows name the same one
- route_gates: float32 [8192, 8], P('expert'), may hold values from 0.1 to 1
- w_gate: bfloat16 [32, 7168, 1024], P('expert', 'dp'), may hold values from -0.0625 to 0.0625
- w_up: bfloat16 [32, 7168, 1024], P('expert', 'dp'), may hold values from -0.0625 to 0.0625
- w_down: bfloat16 [32, 1024, 7168], P('expert', None, 'dp'), may hold values from -0.1875 to 0.1875
- shared_gate: bfloat16 [7168, 1024], P('dp', 'expert'), may hold values from -0.0625 to 0.0625
- shared_up: bfloat16 [7168, 1024], P('dp', 'expert'), may hold values from -0.0625 to 0.0625
- shared_down: bfloat16 [1024, 7168], P('expert', 'dp'), may hold values from -0.1875 to 0.1875
Outputs:
- grad_tokens: bfloat16 [8192, 7168], P('expert', 'dp')
- grad_gate: bfloat16 [32, 7168, 1024], P('expert', 'dp')
- grad_up: bfloat16 [32, 7168, 1024], P('expert', 'dp')
- grad_down: bfloat16 [32, 1024, 7168], P('expert', None, 'dp')
- grad_shared_gate: float32 [7168, 1024], P('dp', 'expert')
- grad_shared_up: float32 [7168, 1024], P('dp', 'expert')
- grad_shared_down: float32 [1024, 7168], P('expert', 'dp')
Inputs may be any that keep to these rules, and one draw needn't show every extreme that they name: `route_ids`: each row names 8 different experts; in each aligned block of 256 rows no expert is named by more than 12 rows, a bound that some block reaches.
All inputs are finite; a program needn't handle non-finite values.
Results may differ from a plain program's by a relative error of at most 0.018.
Values may be sent and summed in bfloat16 or wider, within the bound.
No kernel may reach another device: no remote copies, remote signals or barrier semaphores. Data moves between devices by JAX's collectives and lax.ppermute only.
A program may use at most 128 MiB of HBM per device.

v0:
```python
import jax
import jax.numpy as jnp
from jax import lax
from jax.sharding import PartitionSpec as P

CAP = 12


def silu_parts(pre):
    sigmoid_val = jax.nn.sigmoid(pre)
    return (pre * sigmoid_val, sigmoid_val * (1.0 + pre * (1.0 - sigmoid_val)))


def contract_rows(left, right):
    return lax.dot_general(
        left, right, (((0,), (0,)), ((), ())), preferred_element_type=jnp.float32
    )


def contract_cols(left, right):
    return lax.dot_general(
        left, right, (((1,), (1,)), ((), ())), preferred_element_type=jnp.float32
    )


def hidden_products(part_gate, part_up, part_act):
    silu_val, silu_slope = silu_parts(part_gate)
    activated = (silu_val * part_up).astype(jnp.bfloat16)
    grad_gate_pre = (part_act * part_up * silu_slope).astype(jnp.bfloat16)
    grad_up_pre = (part_act * silu_val).astype(jnp.bfloat16)
    return (activated, grad_gate_pre, grad_up_pre)


def expert_terms(rows_in, rows_grad, weight_gate, weight_up, weight_down):
    part_gate = jnp.dot(rows_in, weight_gate, preferred_element_type=jnp.float32)
    part_up = jnp.dot(rows_in, weight_up, preferred_element_type=jnp.float32)
    part_act = contract_cols(rows_grad, weight_down)
    pre_gate, pre_up, grad_act = lax.psum((part_gate, part_up, part_act), "dp")
    activated, grad_gate_pre, grad_up_pre = hidden_products(pre_gate, pre_up, grad_act)
    back = contract_cols(grad_gate_pre, weight_gate) + contract_cols(grad_up_pre, weight_up)
    return (
        contract_rows(rows_in, grad_gate_pre),
        contract_rows(rows_in, grad_up_pre),
        contract_rows(activated, rows_grad),
        back,
    )


def shards(
    tokens,
    grad_out,
    route_ids,
    route_gates,
    w_gate,
    w_up,
    w_down,
    shared_gate,
    shared_up,
    shared_down,
):
    n_exp = lax.axis_size("expert")
    capacity = CAP
    grad_scale = 1.0 / n_exp
    targets = jnp.arange(n_exp, dtype=jnp.int32)
    matches = route_ids[:, :, None] == targets[None, None, :]
    chosen = jnp.any(matches, axis=1).astype(jnp.int32)
    gate_total = jnp.sum(jnp.where(matches, route_gates[:, :, None], 0.0), axis=1)
    slot_rank = jnp.cumsum(chosen, axis=0) - 1
    slot_ids = jnp.arange(capacity, dtype=jnp.int32)
    placement = (chosen[:, :, None] == 1) & (slot_rank[:, :, None] == slot_ids[None, None, :])
    place_bf = placement.astype(jnp.bfloat16)
    send_in = jnp.einsum(
        "tec,td->ecd", place_bf, tokens, preferred_element_type=jnp.float32
    ).astype(jnp.bfloat16)
    slot_gate = jnp.einsum("tec,te->ec", placement.astype(jnp.float32), gate_total)
    picked_grad = jnp.einsum("tec,td->ecd", place_bf, grad_out, preferred_element_type=jnp.float32)
    send_grad = (slot_gate[:, :, None] * picked_grad).astype(jnp.bfloat16)
    recv_in = lax.all_to_all(send_in, "expert", split_axis=0, concat_axis=0, tiled=True)
    recv_grad = lax.all_to_all(send_grad, "expert", split_axis=0, concat_axis=0, tiled=True)
    width_dev = tokens.shape[1]
    rows_in = recv_in.reshape(n_exp * capacity, width_dev)
    rows_grad = recv_grad.reshape(n_exp * capacity, width_dev)
    part_gate, part_up, part_down, back = expert_terms(
        rows_in, rows_grad, w_gate[0], w_up[0], w_down[0]
    )
    grad_gate = (part_gate * grad_scale).astype(jnp.bfloat16)[None]
    grad_up = (part_up * grad_scale).astype(jnp.bfloat16)[None]
    grad_down = (part_down * grad_scale).astype(jnp.bfloat16)[None]
    back_rows = lax.all_to_all(
        back.astype(jnp.bfloat16).reshape(n_exp, capacity, width_dev),
        "expert",
        split_axis=0,
        concat_axis=0,
        tiled=True,
    )
    routed = jnp.einsum("tec,ecd->td", place_bf, back_rows, preferred_element_type=jnp.float32)
    whole_gate, whole_up, whole_down = (
        lax.all_gather(shared_gate, "expert", axis=1, tiled=True),
        lax.all_gather(shared_up, "expert", axis=1, tiled=True),
        lax.all_gather(shared_down, "expert", axis=0, tiled=True),
    )
    own_gate, own_up, own_down, shared_back = expert_terms(
        tokens, grad_out, whole_gate, whole_up, whole_down
    )
    sum_gate, sum_up, sum_down = (
        lax.psum_scatter(own_gate, "expert", scatter_dimension=1, tiled=True),
        lax.psum_scatter(own_up, "expert", scatter_dimension=1, tiled=True),
        lax.psum_scatter(own_down, "expert", scatter_dimension=0, tiled=True),
    )
    grad_tokens = (shared_back + routed).astype(jnp.bfloat16)
    return (
        grad_tokens,
        grad_gate,
        grad_up,
        grad_down,
        sum_gate * grad_scale,
        sum_up * grad_scale,
        sum_down * grad_scale,
    )


def solution(mesh):
    in_specs = (
        P("expert", "dp"),
        P("expert", "dp"),
        P("expert", None),
        P("expert", None),
        P("expert", "dp", None),
        P("expert", "dp", None),
        P("expert", None, "dp"),
        P("dp", "expert"),
        P("dp", "expert"),
        P("expert", "dp"),
    )
    out_specs = (
        P("expert", "dp"),
        P("expert", "dp", None),
        P("expert", "dp", None),
        P("expert", None, "dp"),
        P("dp", "expert"),
        P("dp", "expert"),
        P("expert", "dp"),
    )
    return jax.shard_map(shards, mesh=mesh, in_specs=in_specs, out_specs=out_specs, check_vma=False)
```

profile of v0, /device:TPU:2, one launch (start us, length us, event | category | flops | bytes accessed | tf_op | source)
XLA Modules:
  0.0 1041.5 jit_solution(9965556063452526038)
XLA Ops:
  7.2 0.7 all-gather.4.cloned.1.call-update
  8.0 0.7 all-gather.6.cloned.1.call-update
  8.7 0.7 fusion.32
  9.4 0.6 reduce-window.6
  10.3 0.8 select_reduce_fusion
  11.5 1.4 fusion.17
  12.9 1.1 copy.36
  14.0 11.5 %all-to-all-start = ((bf16[32,12,896]{2,1,0:T(8,128)(2,1)}), bf16[32,12,896]{2,1,0:T(8,128)(2,1)S(1)}, u32[]{:S(2)}, u32[]{:S(2)}) async-start(bf16[32,12,896]{2,1,0:T(8,128)(2,1)} %copy.36), calls=%async_computation | async-start | bytes 1835008 | tf_op jit(solution)/shard_map/all_to_all | solution.py:79
  25.6 0.7 all-gather.8.cloned.1.call-update
  26.7 1.1 copy.37
  27.8 25.1 %all-to-all-done = bf16[32,12,896]{2,1,0:T(8,128)(2,1)S(1)} async-done(((bf16[32,12,896]{2,1,0:T(8,128)(2,1)}), bf16[32,12,896]{2,1,0:T(8,128)(2,1)S(1)}, u32[]{:S(2)}, u32[]{:S(2)}) %all-to-all-start) | async-done | bytes 688160 | tf_op jit(solution)/shard_map/all_to_all | solution.py:79
  53.0 4.9 all-to-all-start.1
  57.9 1.0 reshape.47
  58.9 28.4 %all-to-all-done.1 = bf16[32,12,896]{2,1,0:T(8,128)(2,1)} async-done(((bf16[32,12,896]{2,1,0:T(8,128)(2,1)}), bf16[32,12,896]{2,1,0:T(8,128)(2,1)}, u32[]{:S(2)}, u32[]{:S(2)}) %all-to-all-start.1) | async-done | bytes 688160 | tf_op jit(solution)/shard_map/all_to_all | solution.py:78
  87.3 1.3 reshape.48
  88.7 2.1 fusion.2
  90.8 2.1 fusion.6
  92.9 2.1 fusion.8
  95.1 1.8 all-gather.4.cloned.1.call-done
  96.9 3.2 fusion.40
  100.1 75.1 %all-gather.6.cloned.1.call-done = bf16[896,1024]{0,1:T(8,128)(2,1)} async-done(((bf16[896,32]{0,1:T(8,128)(2,1)}), bf16[896,1024]{0,1:T(8,128)(2,1)}) %all-gather.6.cloned.1.call-update) | async-done | bytes 1835024 | tf_op jit(solution)/shard_map/all_gather | solution.py:99
  175.2 3.2 fusion.41
  178.4 74.4 %all-gather.8.cloned.1.call-done = bf16[896,1024]{0,1:T(8,128)(2,1)} async-done(((bf16[896,32]{0,1:T(8,128)(2,1)}), bf16[896,1024]{0,1:T(8,128)(2,1)}) %all-gather.8.cloned.1.call-update) | async-done | bytes 1835024 | tf_op jit(solution)/shard_map/all_gather | solution.py:98
  252.8 3.2 fusion.42
  256.1 100.3 %all-reduce.3.cloned.1.call-done = (f32[384,1024]{1,0:T(8,128)}, f32[384,1024]{1,0:T(8,128)}, f32[384,1024]{1,0:T(8,128)}, f32[256,1024]{1,0:T(8,128)}, f32[256,1024]{1,0:T(8,128)}, /*index=5*/f32[256,1024]{1,0:T(8,128)}) async-done(((f32[384,1024]{1,0:T(8,128)}, f32[384,1024]{1,0:T(8,128)}, f32[384,1024]{1,0:T(8,128)}, f32[256,1024]{1,0:T(8,128)}, f32[256,1024]{1,0:T(8,128)}, ...) | async-done | bytes 7864336 | tf_op jit(solution)/shard_map/psum | solution.py:38
  356.4 4.1 fusion.25
  360.6 2.5 multiply_convert_fusion.7
  363.1 2.7 convolution_bitcast_fusion
  366.0 2.6 convolution_bitcast_fusion.1
  368.7 3.3 multiply_convert_fusion.4
  372.0 1.0 fusion
  373.1 0.9 copy-done.17
  374.1 1.9 fusion.18
  375.9 2.1 reshape.49
  378.0 10.2 all-to-all-start.2
  388.3 3.8 fusion.12
  392.1 2.4 fusion.11
  394.5 1.6 fusion.43
  396.7 2.5 fusion.13
  399.3 18.7 %all-to-all-done.2 = bf16[32,12,896]{2,1,0:T(8,128)(2,1)} async-done(((bf16[32,12,896]{2,1,0:T(8,128)(2,1)}), bf16[32,12,896]{2,1,0:T(8,128)(2,1)}, u32[]{:S(2)}, u32[]{:S(2)}) %all-to-all-start.2) | async-done | bytes 688160 | tf_op jit(solution)/shard_map/all_to_all | solution.py:89
  417.9 1.8 convolution_bitcast_fusion.2
  420.0 1.5 fusion.22
  421.5 167.4 %reduce-scatter.8.cloned.1.call-done = f32[32,896]{1,0:T(8,128)} async-done(((f32[1024,896]{1,0:T(8,128)}), f32[32,896]{1,0:T(8,128)}) %reduce-scatter.8.cloned.1.call-update) | async-done | bytes 114704 | tf_op jit(solution)/shard_map/reduce_scatter | solution.py:108
  588.8 1.6 broadcast_multiply_fusion
  590.4 220.8 %reduce-scatter.6.cloned.1.call-done = f32[896,32]{0,1:T(8,128)} async-done(((f32[896,1024]{0,1:T(8,128)}), f32[896,32]{0,1:T(8,128)}) %reduce-scatter.6.cloned.1.call-update) | async-done | bytes 114704 | tf_op jit(solution)/shard_map/reduce_scatter | solution.py:107
  811.2 1.6 broadcast_multiply_fusion.1
  812.8 220.3 %reduce-scatter.4.cloned.1.call-done = f32[896,32]{0,1:T(8,128)} async-done(((f32[896,1024]{0,1:T(8,128)}), f32[896,32]{0,1:T(8,128)}) %reduce-scatter.4.cloned.1.call-update) | async-done | bytes 114704 | tf_op jit(solution)/shard_map/reduce_scatter | solution.py:106
  1033.1 1.6 broadcast_multiply_fusion.2
  (56 shorter events, 2.5 us)
Async XLA Ops:
  7.2 81.5 %copy-start = (bf16[1,896,1024]{2,1,0:T(8,128)(2,1)S(1)}, bf16[1,896,1024]{2,1,0:T(8,128)(2,1)}, u32[]{:S(2)}) copy-start(bf16[1,896,1024]{2,1,0:T(8,128)(2,1)} %param.14) | copy-start | bytes 5505028
  7.2 89.7 %all-gather.4.cloned.1.call-start = ((), (), s32[]{:S(2)}) async-start(), calls=%async_computation.6 | async-start | bytes 1892352 | tf_op jit(solution)/shard_map/all_gather | solution.py:100
  7.9 167.2 %all-gather.6.cloned.1.call-start = ((), (), s32[]{:S(2)}) async-start(), calls=%async_computation.7 | async-start | bytes 1892352 | tf_op jit(solution)/shard_map/all_gather | solution.py:99
  12.9 13.4 %copy-start.1 = (bf16[256,896]{1,0:T(8,128)(2,1)S(1)}, bf16[256,896]{1,0:T(8,128)(2,1)}, u32[]{:S(2)}) copy-start(bf16[256,896]{1,0:T(8,128)(2,1)} %param.10) | copy-start | bytes 1376260
  14.0 38.9 %all-to-all-start = ((bf16[32,12,896]{2,1,0:T(8,128)(2,1)}), bf16[32,12,896]{2,1,0:T(8,128)(2,1)S(1)}, u32[]{:S(2)}, u32[]{:S(2)}) async-start(bf16[32,12,896]{2,1,0:T(8,128)(2,1)} %copy.36), calls=%async_computation | async-start | bytes 1835008 | tf_op jit(solution)/shard_map/all_to_all | solution.py:79
  25.5 227.2 %all-gather.8.cloned.1.call-start = ((), (), s32[]{:S(2)}) async-start(), calls=%async_computation.8 | async-start | bytes 1892352 | tf_op jit(solution)/shard_map/all_gather | solution.py:98
  53.0 34.4 %all-to-all-start.1 = ((bf16[32,12,896]{2,1,0:T(8,128)(2,1)}), bf16[32,12,896]{2,1,0:T(8,128)(2,1)}, u32[]{:S(2)}, u32[]{:S(2)}) async-start(bf16[32,12,896]{2,1,0:T(8,128)(2,1)} %copy.37), calls=%async_computation.1 | async-start | bytes 1835008 | tf_op jit(solution)/shard_map/all_to_all | solution.py:78
  57.9 298.6 %all-reduce.3.cloned.1.call-start = ((), (), s32[]{:S(2)}) async-start(), calls=%async_computation.12 | async-start | bytes 15728640 | tf_op jit(solution)/shard_map/psum | solution.py:38
  88.7 2.1 copy-start.13
  88.7 2.1 copy-start.16
  90.8 2.1 copy-start.11
  90.8 2.1 copy-start.15
  92.9 3.9 copy-start.5
  256.0 332.8 %reduce-scatter.8.cloned.1.call-start = ((), (), s32[]{:S(2)}) async-start(), calls=%async_computation.11 | async-start | bytes 3784704 | tf_op jit(solution)/shard_map/reduce_scatter | solution.py:108
  360.6 450.7 %reduce-scatter.6.cloned.1.call-start = ((), (), s32[]{:S(2)}) async-start(), calls=%async_computation.10 | async-start | bytes 3784704 | tf_op jit(solution)/shard_map/reduce_scatter | solution.py:107
  365.8 667.3 %reduce-scatter.4.cloned.1.call-start = ((), (), s32[]{:S(2)}) async-start(), calls=%async_computation.9 | async-start | bytes 3784704 | tf_op jit(solution)/shard_map/reduce_scatter | solution.py:106
  372.0 1.1 copy-start.8
  372.0 1.1 copy-start.10
  372.0 2.1 copy-start.17
  378.0 39.9 %all-to-all-start.2 = ((bf16[32,12,896]{2,1,0:T(8,128)(2,1)}), bf16[32,12,896]{2,1,0:T(8,128)(2,1)}, u32[]{:S(2)}, u32[]{:S(2)}) async-start(bf16[32,12,896]{2,1,0:T(8,128)(2,1)} %reshape.49), calls=%async_computation.2 | async-start | bytes 1835008 | tf_op jit(solution)/shard_map/all_to_all | solution.py:89
  388.2 3.9 copy-start.9
  388.2 3.9 copy-start.14
  392.1 2.4 copy-start.3
  392.1 4.0 copy-start.12
  394.5 1.7 copy-start.6
  394.5 2.2 copy-start.7
  417.9 1.8 copy-start.2
  417.9 2.0 copy-start.4
Sparse Core Ops, SparseCore 0:
  10.6 86.2 all-gather.3
  99.4 75.6 all-gather.5
  177.7 74.9 all-gather.7
  256.1 100.2 all-reduce.2
  360.7 228.1 reduce-scatter.7
  593.1 218.0 reduce-scatter.5
  815.1 217.9 reduce-scatter.3
where the time goes:
time: 1040 us
  waiting for transfers between devices  934 us (90%)
  matrix products  44 us (4%)
  starting transfers between devices  27.1 us (3%)
  between operations  14.4 us (1%)
  other arithmetic  12.7 us (1%)
    reduce_scatter x1, waiting for transfers between devices, shards(): lax.psum_scatter(own_up, 'expert', scatter_dimension=1, tiled=True)  221 us
    reduce_scatter x1, waiting for transfers between devices, shards(): lax.psum_scatter(own_gate, 'expert', scatter_dimension=1, tiled=True)  220 us
    reduce_scatter x1, waiting for transfers between devices, shards(): lax.psum_scatter(own_down, 'expert', scatter_dimension=0, tiled=True)  167 us
    psum x1, waiting for transfers between devices, expert_terms(): pre_gate, pre_up, grad_act = lax.psum((part_gate, part_up, part_act), 'dp')  100 us
    all_gather x1, waiting for transfers between devices, shards(): lax.all_gather(shared_up, 'expert', axis=1, tiled=True)  75.1 us
    all_gather x1, waiting for transfers between devices, shards(): lax.all_gather(shared_gate, 'expert', axis=1, tiled=True)  74.4 us
    all_to_all x1, waiting for transfers between devices, shards(): lax.all_to_all(send_in, 'expert', split_axis=0, concat_axis=0, tiled=True)  28.4 us
    all_to_all x1, waiting for transfers between devices, shards(): lax.all_to_all(send_grad, 'expert', split_axis=0, concat_axis=0, tiled=True)  25.1 us
  transfers between devices with their start and end apart: 10, of which 10 were waited for; matrix products, arithmetic and copies ran while one was open for 5% of the time, Pallas kernels for 0%

commit v1 on v0

--- a/solution.py
+++ b/solution.py
@@ -4,6 +4,13 @@
 from jax.sharding import PartitionSpec as P
 
 CAP = 12
+
+
+def exchange_gather(x, axis, along):
+    size = lax.axis_size(axis)
+    blocks = jnp.stack([x for _ in range(size)])
+    blocks = lax.all_to_all(blocks, axis, split_axis=0, concat_axis=0)
+    return jnp.concatenate(blocks, axis=along)
 
 
 def silu_parts(pre):
@@ -96,7 +103,7 @@
     routed = jnp.einsum("tec,ecd->td", place_bf, back_rows, preferred_element_type=jnp.float32)
     whole_gate, whole_up, whole_down = (
         lax.all_gather(shared_gate, "expert", axis=1, tiled=True),
-        lax.all_gather(shared_up, "expert", axis=1, tiled=True),
+        exchange_gather(shared_up, "expert", 1),
         lax.all_gather(shared_down, "expert", axis=0, tiled=True),
     )
     own_gate, own_up, own_down, shared_back = expert_terms(

time: 1040 us -> 967 us (0.930)
  waiting for transfers between devices: 934 us -> 822 us
  blocking collectives: 0 us -> 34.6 us
    all_gather x1 -> x0, waiting for transfers between devices: 75.1 us -> none  [shards(): lax.all_gather(shared_up, 'expert', axis=1, tiled=True)]
    all_gather x1, waiting for transfers between devices: 74.4 us -> 33.8 us  [shards(): lax.all_gather(shared_gate, 'expert', axis=1, tiled=True)]
    all_to_all x0 -> x1, blocking collectives: none -> 34.6 us  [shards(): lax.all_to_all(send_in, 'expert', split_axis=0, concat_axis=0, tiled=True)]
  transfers between devices with their start and end apart: 10 -> 9, of which waited for: 10 -> 8; matrix products, arithmetic and copies ran while one was open for 5% -> 6% of each run, Pallas kernels for 0% -> 0%
where the time goes in v1:
time: 967 us; the launch traced here: 966 us
  waiting for transfers between devices  822 us (85%)
  matrix products  45.5 us (5%)
  blocking collectives  34.6 us (4%)
  starting transfers between devices  27.3 us (3%)
  between operations  14.4 us (1%)
  other arithmetic  12.8 us (1%)
  local copies, waits for them, and re-layouts  9.91 us (1%)
    reduce_scatter x1, waiting for transfers between devices, shards(): lax.psum_scatter(own_up, 'expert', scatter_dimension=1, tiled=True)  221 us
    reduce_scatter x1, waiting for transfers between devices, shards(): lax.psum_scatter(own_gate, 'expert', scatter_dimension=1, tiled=True)  220 us
    reduce_scatter x1, waiting for transfers between devices, shards(): lax.psum_scatter(own_down, 'expert', scatter_dimension=0, tiled=True)  166 us
    psum x1, waiting for transfers between devices, expert_terms(): pre_gate, pre_up, grad_act = lax.psum((part_gate, part_up, part_act), 'dp')  100 us
    all_to_all x1, waiting for transfers between devices, exchange_gather(): blocks = lax.all_to_all(blocks, axis, split_axis=0, concat_axis=0)  35 us
    all_to_all x1, blocking collectives, shards(): lax.all_to_all(send_in, 'expert', split_axis=0, concat_axis=0, tiled=True)  34.6 us
    all_gather x1, waiting for transfers between devices, shards(): lax.all_gather(shared_gate, 'expert', axis=1, tiled=True)  33.8 us
    all_to_all x1, waiting for transfers between devices, shards(): lax.all_to_all(send_grad, 'expert', split_axis=0, concat_axis=0, tiled=True)  25.8 us
  transfers between devices with their start and end apart: 9, of which 8 were waited for; matrix products, arithmetic and copies ran while one was open for 6% of the time, Pallas kernels for 0%

profile of v1, /device:TPU:2, one launch (start us, length us, event | category | flops | bytes accessed | tf_op | source)
XLA Modules:
  0.0 966.3 jit_solution(11065181936548942574)
XLA Ops:
  7.2 0.7 all-gather.3.cloned.1.call-update
  7.9 0.7 fusion.32
  8.7 0.7 select_reduce_fusion
  9.4 0.6 reduce-window.6
  10.7 1.4 fusion.17
  12.2 1.1 copy.37
  13.3 11.5 %all-to-all-start.1 = ((bf16[32,12,896]{2,1,0:T(8,128)(2,1)}), bf16[32,12,896]{2,1,0:T(8,128)(2,1)S(1)}, u32[]{:S(2)}, u32[]{:S(2)}) async-start(bf16[32,12,896]{2,1,0:T(8,128)(2,1)} %copy.37), calls=%async_computation.1 | async-start | bytes 1835008 | tf_op jit(solution)/shard_map/all_to_all | solution.py:86
  25.2 1.1 copy.38
  26.3 25.8 %all-to-all-done.1 = bf16[32,12,896]{2,1,0:T(8,128)(2,1)S(1)} async-done(((bf16[32,12,896]{2,1,0:T(8,128)(2,1)}), bf16[32,12,896]{2,1,0:T(8,128)(2,1)S(1)}, u32[]{:S(2)}, u32[]{:S(2)}) %all-to-all-start.1) | async-done | bytes 688160 | tf_op jit(solution)/shard_map/all_to_all | solution.py:86
  52.2 34.6 %all_to_all.20 = bf16[32,12,896]{2,1,0:T(8,128)(2,1)} all-to-all(bf16[32,12,896]{2,1,0:T(8,128)(2,1)} %copy.38), channel_id=1, replica_groups=mesh['dp'=8,'expert'=32] {'expert'}, dimensions={0} | all-to-all | bytes 1376256 | tf_op jit(solution)/shard_map/all_to_all | solution.py:85
  86.7 1.4 stack.2
  88.1 5.2 all-to-all-start
  93.3 0.7 all-gather.5.cloned.1.call-update
  94.1 1.0 reshape.57
  95.1 1.3 reshape.58
  96.4 2.1 fusion.2
  98.6 2.1 fusion.6
  100.7 2.2 fusion.8
  102.8 35.0 %all-to-all-done = bf16[32,896,32]{1,2,0:T(8,128)(2,1)} async-done(((bf16[32,896,32]{1,2,0:T(8,128)(2,1)}), bf16[32,896,32]{1,2,0:T(8,128)(2,1)}, u32[]{:S(2)}, u32[]{:S(2)}) %all-to-all-start) | async-done | bytes 1835040 | tf_op jit(solution)/shard_map/all_to_all | solution.py:12
  137.8 3.3 fusion.41
  141.1 3.2 fusion.40
  144.3 33.8 %all-gather.5.cloned.1.call-done = bf16[896,1024]{0,1:T(8,128)(2,1)} async-done(((bf16[896,32]{0,1:T(8,128)(2,1)}), bf16[896,1024]{0,1:T(8,128)(2,1)}) %all-gather.5.cloned.1.call-update) | async-done | bytes 1835024 | tf_op jit(solution)/shard_map/all_gather | solution.py:105
  178.1 3.2 fusion.42
  181.4 100.4 %all-reduce.3.cloned.1.call-done = (f32[384,1024]{1,0:T(8,128)}, f32[384,1024]{1,0:T(8,128)}, f32[384,1024]{1,0:T(8,128)}, f32[256,1024]{1,0:T(8,128)}, f32[256,1024]{1,0:T(8,128)}, /*index=5*/f32[256,1024]{1,0:T(8,128)}) async-done(((f32[384,1024]{1,0:T(8,128)}, f32[384,1024]{1,0:T(8,128)}, f32[384,1024]{1,0:T(8,128)}, f32[256,1024]{1,0:T(8,128)}, f32[256,1024]{1,0:T(8,128)}, ...) | async-done | bytes 7864336 | tf_op jit(solution)/shard_map/psum | solution.py:45
  281.7 4.1 fusion.25
  285.9 2.5 multiply_convert_fusion.7
  288.4 2.7 convolution_bitcast_fusion
  291.3 2.6 convolution_bitcast_fusion.1
  294.0 3.3 multiply_convert_fusion.4
  297.3 1.0 fusion
  298.4 0.9 copy-done.17
  299.4 1.9 fusion.18
  301.2 2.1 reshape.59
  303.3 10.2 %all-to-all-start.3 = ((bf16[32,12,896]{2,1,0:T(8,128)(2,1)}), bf16[32,12,896]{2,1,0:T(8,128)(2,1)}, u32[]{:S(2)}, u32[]{:S(2)}) async-start(bf16[32,12,896]{2,1,0:T(8,128)(2,1)} %reshape.59), calls=%async_computation.3 | async-start | bytes 1835008 | tf_op jit(solution)/shard_map/all_to_all | solution.py:96
  313.6 3.8 fusion.12
  317.4 2.4 fusion.11
  319.8 1.7 fusion.43
  321.5 0.5 copy-done.6
  322.0 2.5 fusion.13
  324.6 18.7 %all-to-all-done.3 = bf16[32,12,896]{2,1,0:T(8,128)(2,1)} async-done(((bf16[32,12,896]{2,1,0:T(8,128)(2,1)}), bf16[32,12,896]{2,1,0:T(8,128)(2,1)}, u32[]{:S(2)}, u32[]{:S(2)}) %all-to-all-start.3) | async-done | bytes 688160 | tf_op jit(solution)/shard_map/all_to_all | solution.py:96
  343.3 1.7 convolution_bitcast_fusion.2
  345.0 3.0 fusion.22
  348.0 166.1 %reduce-scatter.8.cloned.1.call-done = f32[32,896]{1,0:T(8,128)} async-done(((f32[1024,896]{1,0:T(8,128)}), f32[32,896]{1,0:T(8,128)}) %reduce-scatter.8.cloned.1.call-update) | async-done | bytes 114704 | tf_op jit(solution)/shard_map/reduce_scatter | solution.py:115
  514.0 1.6 broadcast_multiply_fusion
  515.6 220.6 %reduce-scatter.6.cloned.1.call-done = f32[896,32]{0,1:T(8,128)} async-done(((f32[896,1024]{0,1:T(8,128)}), f32[896,32]{0,1:T(8,128)}) %reduce-scatter.6.cloned.1.call-update) | async-done | bytes 114704 | tf_op jit(solution)/shard_map/reduce_scatter | solution.py:114
  736.2 1.6 broadcast_multiply_fusion.1
  737.8 220.1 %reduce-scatter.4.cloned.1.call-done = f32[896,32]{0,1:T(8,128)} async-done(((f32[896,1024]{0,1:T(8,128)}), f32[896,32]{0,1:T(8,128)}) %reduce-scatter.4.cloned.1.call-update) | async-done | bytes 114704 | tf_op jit(solution)/shard_map/reduce_scatter | solution.py:113
  957.9 1.6 broadcast_multiply_fusion.2
  (55 shorter events, 1.7 us)
Async XLA Ops:
  7.2 89.2 %copy-start = (bf16[1,896,1024]{2,1,0:T(8,128)(2,1)S(1)}, bf16[1,896,1024]{2,1,0:T(8,128)(2,1)}, u32[]{:S(2)}) copy-start(bf16[1,896,1024]{2,1,0:T(8,128)(2,1)} %param.14) | copy-start | bytes 5505028
  7.2 133.9 %all-gather.3.cloned.1.call-start = ((), (), s32[]{:S(2)}) async-start(), calls=%async_computation.7 | async-start | bytes 1892352 | tf_op jit(solution)/shard_map/all_gather | solution.py:107
  12.1 12.7 %copy-start.1 = (bf16[256,896]{1,0:T(8,128)(2,1)S(1)}, bf16[256,896]{1,0:T(8,128)(2,1)}, u32[]{:S(2)}) copy-start(bf16[256,896]{1,0:T(8,128)(2,1)} %param.10) | copy-start | bytes 1376260
  13.3 38.9 %all-to-all-start.1 = ((bf16[32,12,896]{2,1,0:T(8,128)(2,1)}), bf16[32,12,896]{2,1,0:T(8,128)(2,1)S(1)}, u32[]{:S(2)}, u32[]{:S(2)}) async-start(bf16[32,12,896]{2,1,0:T(8,128)(2,1)} %copy.37), calls=%async_computation.1 | async-start | bytes 1835008 | tf_op jit(solution)/shard_map/all_to_all | solution.py:86
  25.2 61.5 %copy-start.14 = (bf16[896,32]{0,1:T(8,128)(2,1)S(1)}, bf16[896,32]{0,1:T(8,128)(2,1)}, u32[]{:S(2)}) copy-start(bf16[896,32]{0,1:T(8,128)(2,1)} %param.18) | copy-start | bytes 172036
  88.1 49.7 %all-to-all-start = ((bf16[32,896,32]{1,2,0:T(8,128)(2,1)}), bf16[32,896,32]{1,2,0:T(8,128)(2,1)}, u32[]{:S(2)}, u32[]{:S(2)}) async-start(bf16[32,896,32]{1,2,0:T(8,128)(2,1)} %stack.2), calls=%async_computation | async-start | bytes 3670016 | tf_op jit(solution)/shard_map/all_to_all | solution.py:12
  93.3 84.8 %all-gather.5.cloned.1.call-start = ((), (), s32[]{:S(2)}) async-start(), calls=%async_computation.8 | async-start | bytes 1892352 | tf_op jit(solution)/shard_map/all_gather | solution.py:105
  94.0 187.7 %all-reduce.3.cloned.1.call-start = ((), (), s32[]{:S(2)}) async-start(), calls=%async_computation.12 | async-start | bytes 15728640 | tf_op jit(solution)/shard_map/psum | solution.py:45
  96.4 2.1 copy-start.12
  96.4 2.1 copy-start.16
  98.6 2.1 copy-start.10
  98.6 2.1 copy-start.15
  102.8 38.3 %copy-start.4 = (bf16[256,896]{1,0:T(8,128)(2,1)S(1)}, bf16[256,896]{1,0:T(8,128)(2,1)}, u32[]{:S(2)}) copy-start(bf16[256,896]{1,0:T(8,128)(2,1)} %param.11) | copy-start | bytes 1376260
  181.3 332.7 %reduce-scatter.8.cloned.1.call-start = ((), (), s32[]{:S(2)}) async-start(), calls=%async_computation.11 | async-start | bytes 3784704 | tf_op jit(solution)/shard_map/reduce_scatter | solution.py:115
  285.9 450.3 %reduce-scatter.6.cloned.1.call-start = ((), (), s32[]{:S(2)}) async-start(), calls=%async_computation.10 | async-start | bytes 3784704 | tf_op jit(solution)/shard_map/reduce_scatter | solution.py:114
  291.1 666.7 %reduce-scatter.4.cloned.1.call-start = ((), (), s32[]{:S(2)}) async-start(), calls=%async_computation.9 | async-start | bytes 3784704 | tf_op jit(solution)/shard_map/reduce_scatter | solution.py:113
  297.3 1.1 copy-start.7
  297.3 1.1 copy-start.9
  297.3 2.1 copy-start.17
  303.3 39.9 %all-to-all-start.3 = ((bf16[32,12,896]{2,1,0:T(8,128)(2,1)}), bf16[32,12,896]{2,1,0:T(8,128)(2,1)}, u32[]{:S(2)}, u32[]{:S(2)}) async-start(bf16[32,12,896]{2,1,0:T(8,128)(2,1)} %reshape.59), calls=%async_computation.3 | async-start | bytes 1835008 | tf_op jit(solution)/shard_map/all_to_all | solution.py:96
  313.5 3.9 copy-start.8
  313.5 3.9 copy-start.13
  317.4 2.4 copy-start.2
  317.4 4.1 copy-start.11
  319.8 1.7 copy-start.5
  319.8 2.2 copy-start.6
  343.2 1.7 copy-start.3
Sparse Core Ops, SparseCore 0:
  10.6 85.5 all-gather.2
  98.8 79.2 all-gather.4
  181.5 100.2 all-reduce.2
  286.0 228.0 reduce-scatter.7
  518.3 217.8 reduce-scatter.5
  739.9 217.8 reduce-scatter.3
